TPU v7x, 32 devices: a whole 2x2x4 slice. The times are simulated.
32 devices in a mesh: fac: 2 (over core), str: 16 (over z, y, x).
Axes of the slice: x: 2, y: 2, z: 4, core: 2. Of those that a mesh axis runs over, the one named last changes fastest.
Arguments:
- vector: bfloat16 [4096, 8192], P('str'), may hold values from -6 to 6
- alpha_tiles: bfloat16 [2, 4, 128, 128], P('fac'), may hold values from -0.25 to 0.25
- alpha_pattern: int32 [2, 32, 4], P('fac'), may hold values from 0 to 31
- beta_tiles: bfloat16 [2, 4, 128, 128], P('fac'), may hold values from -0.25 to 0.25
- beta_pattern: int32 [2, 64, 4], P('fac'), may hold values from 0 to 63
- alpha_sector: int32 [32], replicated, may hold values from 0 to 1
- beta_sector: int32 [64], replicated, may hold values from 0 to 1
- alpha_diag: float32 [4096], replicated, may hold values from 0.5 to 2
- beta_diag: float32 [8192], replicated, may hold values from 0.5 to 2
- energy: float32 [1], replicated, may hold values from -1 to 0
Outputs:
- first_update: bfloat16 [4096, 8192], P('fac', 'str')
- second_update: bfloat16 [4096, 8192], P('str', 'fac')
All inputs are finite; a program needn't handle non-finite values.
Results may differ from a plain program's by a relative error of at most 0.0064.
Values may be sent and summed in bfloat16 or wider, within the bound.
A program may use at most 128 MiB of HBM per device.

v0:
```python
import jax
import jax.numpy as jnp
from jax import lax
from jax.sharding import PartitionSpec as P


def beta_apply(matrix, tile_set, pattern):
    height = matrix.shape[0]
    slot_count = tile_set.shape[0]
    block_size = tile_set.shape[1]
    count_blocks = matrix.shape[1] // block_size
    blocks = matrix.reshape(height, count_blocks, block_size)
    picked = jnp.take(blocks, pattern.reshape(-1), axis=1).reshape(
        height, count_blocks, slot_count * block_size
    )
    stacked = tile_set.reshape(slot_count * block_size, block_size)
    result = jnp.einsum("rjk,kc->rjc", picked, stacked, preferred_element_type=jnp.float32)
    return result.reshape(height, count_blocks * block_size)


def alpha_apply(matrix, tile_set, pattern):
    breadth = matrix.shape[1]
    slot_count = tile_set.shape[0]
    block_size = tile_set.shape[1]
    count_blocks = matrix.shape[0] // block_size
    blocks = matrix.reshape(count_blocks, block_size, breadth)
    picked = jnp.take(blocks, pattern.reshape(-1), axis=0).reshape(
        count_blocks, slot_count * block_size, breadth
    )
    stacked = tile_set.transpose(1, 0, 2).reshape(block_size, slot_count * block_size)
    result = jnp.einsum("ak,jkc->jac", stacked, picked, preferred_element_type=jnp.float32)
    return result.reshape(count_blocks * block_size, breadth)


def precondition(
    sigma_part,
    row_start,
    col_start,
    block_size,
    alpha_sector,
    beta_sector,
    alpha_diag,
    beta_diag,
    energy,
):
    row_count, col_count = sigma_part.shape
    row_blocks = row_count // block_size
    col_blocks = col_count // block_size
    alpha_labels = lax.dynamic_slice_in_dim(alpha_sector, row_start // block_size, row_blocks)
    beta_labels = lax.dynamic_slice_in_dim(beta_sector, col_start // block_size, col_blocks)
    live_mask = (alpha_labels[:, None, None, None] == beta_labels[None, None, :, None]).astype(
        jnp.float32
    )
    masked = (
        sigma_part.reshape(row_blocks, block_size, col_blocks, block_size) * live_mask
    ).reshape(row_count, col_count)
    alpha_part = lax.dynamic_slice_in_dim(alpha_diag, row_start, row_count)
    beta_part = lax.dynamic_slice_in_dim(beta_diag, col_start, col_count)
    denominator = alpha_part[:, None] + beta_part[None, :] - energy[0]
    return (masked / denominator).astype(jnp.bfloat16)


def body(
    vector,
    alpha_tiles,
    alpha_pattern,
    beta_tiles,
    beta_pattern,
    alpha_sector,
    beta_sector,
    alpha_diag,
    beta_diag,
    energy,
):
    string_index = lax.axis_index("str")
    group_index = lax.axis_index("fac")
    string_count = lax.axis_size("str")
    block_size = alpha_tiles.shape[2]
    row_count = vector.shape[0]
    col_count = vector.shape[1] // string_count
    factor = 0
    image = beta_apply(vector, beta_tiles[factor], beta_pattern[factor]).astype(jnp.bfloat16)
    moved_one = lax.all_to_all(image, "str", split_axis=1, concat_axis=0, tiled=True)
    partial_value = alpha_apply(moved_one, alpha_tiles[factor], alpha_pattern[factor])
    share_rows = lax.psum_scatter(partial_value, "fac", scatter_dimension=0, tiled=True)
    first_update = precondition(
        share_rows,
        group_index * share_rows.shape[0],
        string_index * col_count,
        block_size,
        alpha_sector,
        beta_sector,
        alpha_diag,
        beta_diag,
        energy,
    )
    whole_first = lax.all_gather(first_update, "fac", axis=0, tiled=True)
    factor = 0
    back_image = alpha_apply(whole_first, alpha_tiles[factor], alpha_pattern[factor]).astype(
        jnp.bfloat16
    )
    returned_one = lax.all_to_all(back_image, "str", split_axis=0, concat_axis=1, tiled=True)
    partial_back = beta_apply(returned_one, beta_tiles[factor], beta_pattern[factor])
    share_cols = lax.psum_scatter(partial_back, "fac", scatter_dimension=1, tiled=True)
    second_update = precondition(
        share_cols,
        string_index * row_count,
        group_index * share_cols.shape[1],
        block_size,
        alpha_sector,
        beta_sector,
        alpha_diag,
        beta_diag,
        energy,
    )
    return (first_update, second_update)


def solution(mesh):
    return jax.shard_map(
        body,
        mesh=mesh,
        in_specs=(
            P("str", None),
            P("fac", None, None, None),
            P("fac", None, None),
            P("fac", None, None, None),
            P("fac", None, None),
            P(),
            P(),
            P(),
            P(),
            P(),
        ),
        out_specs=(P("fac", "str"), P("str", "fac")),
        check_vma=False,
    )
```

profile of v0, /device:TPU:3, one launch (start us, length us, event | category | flops | bytes accessed | tf_op | source)
XLA Modules:
  0.0 485.7 jit_solution(11953239755636948824)
XLA Ops:
  7.2 0.8 copy.32
  8.0 0.1 reshape_squeeze.12
  8.1 6.4 %copy.33 = bf16[256,8192]{0,1:T(8,128)(2,1)} copy(bf16[256,8192]{1,0:T(8,128)(2,1)} %param.14) | data formatting | bytes 8388608 | tf_op args[0]
  14.6 6.4 %copy.34 = bf16[256,64,128]{2,0,1:T(8,128)(2,1)} copy(bf16[256,64,128]{0,2,1:T(8,128)(2,1)} %bitcast.77) | data formatting | bytes 8388608 | tf_op jit(solution)/shard_map/reshape | solution.py:12
  20.9 11.9 %gather_fusion = bf16[256,256,128]{2,1,0:T(8,128)(2,1)} fusion(bf16[256,64,128]{2,0,1:T(8,128)(2,1)} %copy.34, s32[1024]{0:T(1024)S(1)} %pad_clamp_fusion.1), kind=kCustom, calls=%fused_computation.clone | custom fusion | bytes 33555456 | tf_op jit(solution)/shard_map/jit(_take)/gather | solution.py:13
  32.9 14.2 %select_bitcast_fusion.1 = bf16[256,256,128]{2,0,1:T(8,128)(2,1)} fusion(bf16[256,256,128]{2,1,0:T(8,128)(2,1)} %gather_fusion, pred[256]{0:T(512)(128)(4,1)S(1)} %compare_and_fusion.1), kind=kLoop, calls=%fused_computation.5 | loop fusion | flops 8388608 | bytes 33554688 | tf_op jit(solution)/shard_map/jit(_take)/select_n | solution.py:13
  47.0 22.3 %copy.35 = bf16[256,256,128]{0,2,1:T(8,128)(2,1)} copy(bf16[256,256,128]{2,0,1:T(8,128)(2,1)} %select_bitcast_fusion.1) | data formatting | bytes 33554432 | tf_op jit(solution)/shard_map/jit(_take)/select_n | solution.py:13
  69.3 10.2 %convolution_convert_fusion.1 = bf16[256,64,128]{0,2,1:T(8,128)(2,1)} fusion(bf16[256,64,512]{0,2,1:T(8,128)(2,1)} %bitcast.65, bf16[512,128,1]{1,0,2:T(8,128)(2,1)S(1)} %bitcast.63), kind=kOutput, calls=%fused_computation.15 | convolution fusion | flops 2149580800 | bytes 21102592 | tf_op jit(solution)/shard_map/rjk,kc->rjc/dot_general | solution.py:17
  79.5 6.5 %copy.38 = bf16[256,16,512]{2,0,1:T(8,128)(2,1)} copy(bf16[256,16,512]{0,2,1:T(8,128)(2,1)} %bitcast.72) | data formatting | bytes 8388608 | tf_op jit(solution)/shard_map/convert_element_type | solution.py:82
  86.0 6.7 %all-to-all-start = ((bf16[256,16,512]{2,0,1:T(8,128)(2,1)}), bf16[256,16,512]{2,0,1:T(8,128)(2,1)}, u32[]{:S(2)}, u32[]{:S(2)}) async-start(bf16[256,16,512]{2,0,1:T(8,128)(2,1)} %copy.38), calls=%async_computation | async-start | bytes 8388608 | tf_op jit(solution)/shard_map/all_to_all | solution.py:83
  92.7 0.0 reduce-scatter.3.cloned.1.call-start
  92.8 0.1 copy.31
  92.9 0.1 reshape_squeeze.14
  93.0 0.1 copy.39
  93.2 79.1 %all-to-all-done = bf16[256,16,512]{2,0,1:T(8,128)(2,1)} async-done(((bf16[256,16,512]{2,0,1:T(8,128)(2,1)}), bf16[256,16,512]{2,0,1:T(8,128)(2,1)}, u32[]{:S(2)}, u32[]{:S(2)}) %all-to-all-start) | async-done | bytes 4194336 | tf_op jit(solution)/shard_map/all_to_all | solution.py:83
  172.3 10.5 %gather_fusion.1 = bf16[128,128,512]{2,1,0:T(8,128)(2,1)} fusion(bf16[32,128,512]{2,1,0:T(8,128)(2,1)} %bitcast.7, s32[1024]{0:T(1024)S(1)} %pad_clamp_fusion), kind=kCustom, calls=%fused_computation.1.clone | custom fusion | bytes 33554944 | tf_op jit(solution)/shard_map/jit(_take)/gather | solution.py:27
  182.8 8.5 %broadcast_select_fusion.1 = bf16[128,128,512]{2,1,0:T(8,128)(2,1)S(1)} fusion(bf16[128,128,512]{2,1,0:T(8,128)(2,1)} %gather_fusion.1, pred[128]{0:T(512)(128)(4,1)S(1)} %compare_and_fusion), kind=kLoop, calls=%fused_computation.7 | loop fusion | flops 8388608 | bytes 33554560 | tf_op jit(solution)/shard_map/jit(_take)/select_n | solution.py:27
  191.3 6.6 %fusion.4 = f32[32,512,128]{1,2,0:T(8,128)} fusion(bf16[32,512,512]{2,1,0:T(8,128)(2,1)S(1)} %bitcast.68, bf16[128,512,1]{0,1,2:T(8,128)(2,1)S(1)} %bitcast.78), kind=kOutput, calls=%fused_computation.24 | convolution fusion | flops 2147483648 | bytes 25296896 | tf_op jit(solution)/shard_map/ak,jkc->jac/dot_general | solution.py:31
  197.9 0.0 reduce-scatter.3.cloned.1.call-update
  198.0 0.0 all-gather.2.cloned.1.call-start
  198.7 0.1 dynamic_slice.25
  198.8 0.1 dynamic_slice.24
  198.9 0.1 dynamic_slice.27
  199.0 0.1 compare_convert_fusion
  199.0 31.0 %reduce-scatter.3.cloned.1.call-done = f32[2048,512]{1,0:T(8,128)} async-done(((f32[4096,512]{1,0:T(8,128)}), f32[2048,512]{1,0:T(8,128)}) %reduce-scatter.3.cloned.1.call-update) | async-done | bytes 4194320 | tf_op jit(solution)/shard_map/reduce_scatter | solution.py:85
  230.1 0.6 mul.36
  230.7 3.6 fusion.3
  234.3 0.0 all-gather.2.cloned.1.call-update
  234.3 0.2 reduce-scatter.5.cloned.1.call-start
  234.6 14.9 %all-gather.2.cloned.1.call-done = bf16[4096,512]{1,0:T(8,128)(2,1)} async-done(((bf16[2048,512]{1,0:T(8,128)(2,1)}), bf16[4096,512]{1,0:T(8,128)(2,1)}) %all-gather.2.cloned.1.call-update) | async-done | bytes 4194320 | tf_op jit(solution)/shard_map/all_gather | solution.py:97
  249.5 10.5 %gather_fusion.2 = bf16[128,128,512]{2,1,0:T(8,128)(2,1)} fusion(bf16[32,128,512]{2,1,0:T(8,128)(2,1)} %bitcast.69, s32[1024]{0:T(1024)S(1)} %pad_clamp_fusion), kind=kCustom, calls=%fused_computation.3.clone | custom fusion | bytes 33554944 | tf_op jit(solution)/shard_map/jit(_take)/gather | solution.py:27
  260.0 8.5 %broadcast_select_fusion = bf16[128,128,512]{2,1,0:T(8,128)(2,1)S(1)} fusion(bf16[128,128,512]{2,1,0:T(8,128)(2,1)} %gather_fusion.2, pred[128]{0:T(512)(128)(4,1)S(1)} %compare_and_fusion), kind=kLoop, calls=%fused_computation.6 | loop fusion | flops 8388608 | bytes 33554560 | tf_op jit(solution)/shard_map/jit(_take)/select_n | solution.py:27
  268.5 5.2 %convolution_convert_fusion = bf16[32,512,128]{1,2,0:T(8,128)(2,1)} fusion(bf16[32,512,512]{2,1,0:T(8,128)(2,1)S(1)} %bitcast.66, bf16[128,512,1]{0,1,2:T(8,128)(2,1)S(1)} %bitcast.79), kind=kOutput, calls=%fused_computation.14 | convolution fusion | flops 2149580800 | bytes 21102592 | tf_op jit(solution)/shard_map/ak,jkc->jac/dot_general | solution.py:31
  273.7 6.4 %copy.42 = bf16[16,256,512]{1,2,0:T(8,128)(2,1)} copy(bf16[16,256,512]{2,1,0:T(8,128)(2,1)} %bitcast.73) | data formatting | bytes 8388608 | tf_op jit(solution)/shard_map/convert_element_type | solution.py:99
  280.1 97.5 %all_to_all.26 = bf16[16,256,512]{1,2,0:T(8,128)(2,1)} all-to-all(bf16[16,256,512]{1,2,0:T(8,128)(2,1)} %copy.42), channel_id=1, replica_groups=mesh['fac'=2,'str'=16] {'str'}, dimensions={0} | all-to-all | bytes 8388608 | tf_op jit(solution)/shard_map/all_to_all | solution.py:102
  377.6 6.4 %copy.43 = bf16[256,64,128]{2,0,1:T(8,128)(2,1)} copy(bf16[256,64,128]{0,2,1:T(8,128)(2,1)} %bitcast.76) | data formatting | bytes 8388608 | tf_op jit(solution)/shard_map/reshape | solution.py:12
  384.0 11.9 %gather_fusion.3 = bf16[256,256,128]{2,1,0:T(8,128)(2,1)} fusion(bf16[256,64,128]{2,0,1:T(8,128)(2,1)} %copy.43, s32[1024]{0:T(1024)S(1)} %pad_clamp_fusion.1), kind=kCustom, calls=%fused_computation.2.clone | custom fusion | bytes 33555456 | tf_op jit(solution)/shard_map/jit(_take)/gather | solution.py:13
  395.9 14.2 %select_bitcast_fusion = bf16[256,256,128]{2,0,1:T(8,128)(2,1)} fusion(bf16[256,256,128]{2,1,0:T(8,128)(2,1)} %gather_fusion.3, pred[256]{0:T(512)(128)(4,1)S(1)} %compare_and_fusion.1), kind=kLoop, calls=%fused_computation.4 | loop fusion | flops 8388608 | bytes 33554688 | tf_op jit(solution)/shard_map/jit(_take)/select_n | solution.py:13
  410.1 22.3 %copy.44 = bf16[256,256,128]{0,2,1:T(8,128)(2,1)} copy(bf16[256,256,128]{2,0,1:T(8,128)(2,1)} %select_bitcast_fusion) | data formatting | bytes 33554432 | tf_op jit(solution)/shard_map/jit(_take)/select_n | solution.py:13
  432.3 11.6 %fusion.5 = f32[256,64,128]{0,2,1:T(8,128)} fusion(bf16[256,64,512]{0,2,1:T(8,128)(2,1)} %bitcast.67, bf16[512,128,1]{1,0,2:T(8,128)(2,1)S(1)} %bitcast.64), kind=kOutput, calls=%fused_computation.25 | convolution fusion | flops 2147483648 | bytes 25296896 | tf_op jit(solution)/shard_map/rjk,kc->rjc/dot_general | solution.py:17
  443.9 8.9 %copy.47 = f32[256,8192]{1,0:T(8,128)} copy(f32[256,8192]{0,1:T(8,128)} %bitcast.70) | data formatting | bytes 16777216 | tf_op jit(solution)/shard_map/reshape | solution.py:18
  452.9 0.1 dynamic_slice.29
  453.0 0.1 dynamic_slice.28
  453.1 0.1 dynamic_slice.30
  453.1 0.1 compare_convert_fusion.1
  453.2 18.1 %reduce-scatter.5.cloned.1.call-done = f32[256,4096]{1,0:T(8,128)} async-done(((f32[256,8192]{1,0:T(8,128)}), f32[256,4096]{1,0:T(8,128)}) %reduce-scatter.5.cloned.1.call-update) | async-done | bytes 4194320 | tf_op jit(solution)/shard_map/reduce_scatter | solution.py:104
  471.3 0.6 mul.41
  471.9 7.3 %fusion.1 = bf16[256,4096]{1,0:T(8,128)(2,1)} fusion(f32[256,4096]{1,0:T(8,128)} %reduce-scatter.5.cloned.1.call-done, f32[32,8,32,128]{3,2,1,0:T(8,128)S(1)} %bitcast.75, f32[]{:T(128)} %bitcast.62, f32[4096]{0:T(1024)S(1)} %dynamic_slice.31, f32[256]{0:T(256)S(1)} %dynamic_slice.30), kind=kLoop, calls=%fused_computation.10 | loop fusion | flops 5242880 | bytes 10503172 | tf_op jit(solution)/shard_map/convert_element_type | solution.py:60
  (23 shorter events, 0.1 us)
Async XLA Ops:
  7.2 62.2 %copy-start = (bf16[1,4,128,128]{3,2,1,0:T(8,128)(2,1)S(1)}, bf16[1,4,128,128]{3,2,1,0:T(8,128)(2,1)}, u32[]{:S(2)}) copy-start(bf16[1,4,128,128]{3,2,1,0:T(8,128)(2,1)} %param.17) | copy-start | bytes 393220
  79.5 13.3 %copy-start.4 = (s32[1,32,4]{1,2,0:T(4,128)S(1)}, s32[1,32,4]{1,2,0:T(4,128)}, u32[]{:S(2)}) copy-start(s32[1,32,4]{1,2,0:T(4,128)} %param.16) | copy-start | bytes 1540
  79.5 13.5 %copy-start.1 = (bf16[1,4,128,128]{3,2,1,0:T(8,128)(2,1)S(1)}, bf16[1,4,128,128]{3,2,1,0:T(8,128)(2,1)}, u32[]{:S(2)}) copy-start(bf16[1,4,128,128]{3,2,1,0:T(8,128)(2,1)} %param.15) | copy-start | bytes 393220
  86.0 86.3 %all-to-all-start = ((bf16[256,16,512]{2,0,1:T(8,128)(2,1)}), bf16[256,16,512]{2,0,1:T(8,128)(2,1)}, u32[]{:S(2)}, u32[]{:S(2)}) async-start(bf16[256,16,512]{2,0,1:T(8,128)(2,1)} %copy.38), calls=%async_computation | async-start | bytes 8388608 | tf_op jit(solution)/shard_map/all_to_all | solution.py:83
  92.7 137.3 %reduce-scatter.3.cloned.1.call-start = ((), (), s32[]{:S(2)}) async-start(), calls=%async_computation.4 | async-start | bytes 12582912 | tf_op jit(solution)/shard_map/reduce_scatter | solution.py:85
  197.9 0.8 copy-start.5
  197.9 0.9 copy-start.6
  197.9 0.9 copy-start.2
  197.9 1.0 copy-start.3
  198.0 51.5 %all-gather.2.cloned.1.call-start = ((), (), s32[]{:S(2)}) async-start(), calls=%async_computation.5 | async-start | bytes 6291456 | tf_op jit(solution)/shard_map/all_gather | solution.py:97
  234.3 237.0 %reduce-scatter.5.cloned.1.call-start = ((), (), s32[]{:S(2)}) async-start(), calls=%async_computation.6 | async-start | bytes 12582912 | tf_op jit(solution)/shard_map/reduce_scatter | solution.py:104
Sparse Core Ops, SparseCore 0:
  198.1 31.9 reduce-scatter.2
  234.5 14.9 all-gather.1
  453.0 18.2 reduce-scatter.4
where the time goes:
time: 489 us; the launch traced here: 486 us
  waiting for transfers between devices  143 us (29%)
  local copies, waits for them, and re-layouts  133 us (27%)
  blocking collectives  97.5 us (20%)
  other arithmetic  56.5 us (12%)
  matrix products  33.5 us (7%)
  between operations  14.6 us (3%)
  starting transfers between devices  7.05 us (1%)
    all_to_all x1, blocking collectives, body(): lax.all_to_all(back_image, 'str', split_axis=0, concat_axis=1, tiled=True)  97.5 us
    all_to_all x1, waiting for transfers between devices, body(): lax.all_to_all(image, 'str', split_axis=1, concat_axis=0, tiled=True)  79.1 us
    select_n x2, local copies, waits for them, and re-layouts, beta_apply(): jnp.take(blocks, pattern.reshape(-1), axis=1)  44.5 us
    reduce_scatter x1, waiting for transfers between devices, body(): lax.psum_scatter(partial_value, 'fac', scatter_dimension=0, tiled=True)  31 us
    select_n x3, other arithmetic, beta_apply(): jnp.take(blocks, pattern.reshape(-1), axis=1)  28.3 us
    gather x2, local copies, waits for them, and re-layouts, beta_apply(): jnp.take(blocks, pattern.reshape(-1), axis=1)  23.9 us
    dot_general x2, matrix products, beta_apply(): jnp.einsum('rjk,kc->rjc', picked, stacked, preferred_element_type=jnp.flo...  21.8 us
    gather x2, local copies, waits for them, and re-layouts, alpha_apply(): jnp.take(blocks, pattern.reshape(-1), axis=0)  21 us
  transfers between devices with their start and end apart: 4, of which 4 were waited for; matrix products, arithmetic and copies ran while one was open for 0% of the time, Pallas kernels for 0%

commit v1 on v0

--- a/solution.py
+++ b/solution.py
@@ -1,7 +1,13 @@
+import functools
+
 import jax
 import jax.numpy as jnp
 from jax import lax
+from jax.experimental import pallas as pl
+from jax.experimental.pallas import tpu as pltpu
 from jax.sharding import PartitionSpec as P
+
+MESH = pl.DeviceIdType.MESH
 
 
 def beta_apply(matrix, tile_set, pattern):
@@ -116,9 +122,396 @@
     return (first_update, second_update)
 
 
+def exchange_kernel(
+    sizes,
+    vec,
+    ta,
+    tb,
+    pa,
+    pa_slot,
+    pb,
+    pb_slot,
+    live,
+    adiag,
+    bdiag,
+    energy,
+    out1,
+    out2,
+    held,
+    send1,
+    recv1,
+    first,
+    send2,
+    recv2,
+    staged,
+    send1_sem,
+    recv1_sem,
+    send2_sem,
+    recv2_sem,
+    o1_send,
+    o1_recv,
+    o2_send,
+    o2_recv,
+    held_sem,
+):
+    n, nf, bs, kc, sc, qc, nab, nbb = sizes
+    me = lax.axis_index("str")
+    c = lax.axis_index("fac")
+    everyone = n * nf
+    row_blocks = nab // n
+    half_rows = nab // nf
+    half_blocks = nbb // nf
+
+    def partner(slot):
+        return lax.rem(me + slot // nf, n), lax.rem(c + lax.rem(slot, nf), nf)
+
+    def load(b, carry):
+        columns = pl.ds(pl.multiple_of(b * bs, bs), bs)
+        pltpu.make_async_copy(vec.at[:, columns], held.at[b], held_sem).start()
+        return carry
+
+    lax.fori_loop(0, nbb, load, 0)
+    barrier = pltpu.get_barrier_semaphore()
+
+    def greet(slot, carry):
+        d, f = partner(slot)
+        pl.semaphore_signal(
+            barrier, inc=1, device_id={"fac": f, "str": d}, device_id_type=MESH
+        )
+        return carry
+
+    lax.fori_loop(1, everyone, greet, 0)
+    pl.semaphore_wait(barrier, everyone - 1)
+
+    pltpu.make_async_copy(held, held, held_sem).wait()
+
+    def column(ref, index):
+        return jnp.transpose(jnp.broadcast_to(ref[pl.ds(index, 1), :], (bs, bs)))
+
+    def beta_image(q, r, dst):
+        d = lax.rem(me + r, n)
+        j = (d * nf + c) * qc + q
+        for k in range(kc):
+            picked = jnp.concatenate(
+                [
+                    held[pb[(k * nbb + j) * sc + s]] for s in range(sc)
+                ],
+                axis=1,
+            )
+            image = jnp.dot(
+                picked,
+                tb[k * sc * bs : (k + 1) * sc * bs, :],
+                preferred_element_type=jnp.float32,
+            )
+            for x in range(row_blocks):
+                dst[x, k] = image[x * bs : (x + 1) * bs].astype(jnp.bfloat16)
+
+    def first_slot(t):
+        return 1 + lax.rem(t + n // 2 - 1, n - 1)
+
+    def first_copy(q, t):
+        r = first_slot(t)
+        return pltpu.make_async_remote_copy(
+            src_ref=send1[q].at[pl.ds(r * row_blocks, row_blocks)],
+            dst_ref=recv1[q].at[pl.ds(r * row_blocks, row_blocks)],
+            send_sem=send1_sem.at[q],
+            recv_sem=recv1_sem.at[q],
+            device_id={"fac": c, "str": lax.rem(me + r, n)},
+            device_id_type=MESH,
+        )
+
+    for q in range(qc):
+
+        def step_one(t, carry, q=q):
+            r = first_slot(t)
+            beta_image(q, r, send1[q].at[pl.ds(r * row_blocks, row_blocks)])
+
+            @pl.when(t > 0)
+            def _():
+                first_copy(q, t - 1).start()
+
+            return carry
+
+        lax.fori_loop(0, n - 1, step_one, 0)
+        beta_image(q, 0, recv1[q].at[pl.ds(0, row_blocks)])
+        first_copy(q, n - 2).start()
+
+    def second_slot(t):
+        return 1 + lax.rem(t + everyone // 2 - 1, everyone - 1)
+
+    def second_copy(q, t):
+        slot = second_slot(t)
+        d, f = partner(slot)
+        return pltpu.make_async_remote_copy(
+            src_ref=send2[q].at[slot],
+            dst_ref=recv2.at[q * everyone + slot],
+            send_sem=send2_sem.at[q],
+            recv_sem=recv2_sem.at[q],
+            device_id={"fac": f, "str": d},
+            device_id_type=MESH,
+        )
+
+    def share_copy(q, e):
+        f = lax.rem(c + e, nf)
+        src = first[q].at[pl.ds(f * half_rows, half_rows)]
+        dst = out1.at[:, :, pl.ds(pl.multiple_of((c * qc + q) * bs, bs), bs)]
+        if e == 0:
+            return pltpu.make_async_copy(src, dst, o1_send.at[q, e])
+        return pltpu.make_async_remote_copy(
+            src_ref=src,
+            dst_ref=dst,
+            send_sem=o1_send.at[q, e],
+            recv_sem=o1_recv.at[q, e],
+            device_id={"fac": f, "str": me},
+            device_id_type=MESH,
+        )
+
+    for q in range(qc):
+        landed = recv1[q].at[pl.ds(row_blocks, (n - 1) * row_blocks)]
+        pltpu.make_async_copy(landed, landed, recv1_sem.at[q]).wait()
+        j = (me * nf + c) * qc + q
+
+        def sigma_one(i, carry, q=q, j=j):
+            parts = []
+            for k in range(kc):
+                for s in range(sc):
+                    parts.append(recv1[q][pa_slot[(k * nab + i) * sc + s], k])
+            tiles = jnp.concatenate([ta[x] for x in range(kc * sc)], axis=1)
+            sigma = jnp.dot(
+                tiles, jnp.concatenate(parts, axis=0), preferred_element_type=jnp.float32
+            )
+            denominator = column(adiag, i) + bdiag[pl.ds(j, 1), :] - energy[0]
+            value = (sigma * live[i * nbb + j] / denominator).astype(jnp.bfloat16)
+            first[q][i] = value
+            return carry
+
+        lax.fori_loop(0, nab, sigma_one, 0)
+
+        def alpha_image(slot, dst, q=q):
+            d, f = partner(slot)
+            i = d * nf + f
+            for k in range(kc):
+                picked = jnp.concatenate(
+                    [
+                        first[q][pa[(k * nab + i) * sc + s]] for s in range(sc)
+                    ],
+                    axis=0,
+                )
+                tiles = jnp.concatenate([ta[k * sc + s] for s in range(sc)], axis=1)
+                image = jnp.dot(tiles, picked, preferred_element_type=jnp.float32)
+                dst[k] = image.astype(jnp.bfloat16)
+
+        def step_two(t, carry, q=q, alpha_image=alpha_image):
+            slot = second_slot(t)
+            alpha_image(slot, send2[q].at[slot])
+
+            @pl.when(t > 0)
+            def _():
+                second_copy(q, t - 1).start()
+
+            return carry
+
+        lax.fori_loop(0, everyone - 1, step_two, 0)
+        alpha_image(0, recv2.at[q * everyone])
+        second_copy(q, everyone - 2).start()
+        for e in range(nf):
+            share_copy(q, e).start()
+
+    for q in range(qc):
+        landed = recv2.at[pl.ds(q * everyone + 1, everyone - 1)]
+        pltpu.make_async_copy(landed, landed, recv2_sem.at[q]).wait()
+
+    own = me * nf + c
+    alpha_part = column(adiag, own)
+    group = 4 if half_blocks % 4 == 0 else 1
+
+    def sigma_two(first_block):
+        rows = []
+        for g in range(group):
+            parts = []
+            for k in range(kc):
+                for s in range(sc):
+                    slot = pb_slot[(k * nbb + first_block + g) * sc + s]
+                    parts.append(recv2[slot, k])
+            rows.append(jnp.concatenate(parts, axis=1))
+        sigma = jnp.dot(
+            jnp.concatenate(rows, axis=0), tb[...], preferred_element_type=jnp.float32
+        )
+        for g in range(group):
+            j = first_block + g
+            denominator = alpha_part + bdiag[pl.ds(j, 1), :] - energy[0]
+            value = sigma[g * bs : (g + 1) * bs] * live[own * nbb + j] / denominator
+            staged[:, pl.ds(pl.multiple_of(j * bs, bs), bs)] = value.astype(jnp.bfloat16)
+
+    piece = group * (2 if half_blocks % (2 * group) == 0 else 1)
+    pieces = half_blocks // piece
+
+    def piece_copy(e, x):
+        f = lax.rem(c + e, nf)
+        src_start = pl.multiple_of((f * half_blocks + x * piece) * bs, bs)
+        dst_start = pl.multiple_of(x * piece * bs, bs)
+        src = staged.at[:, pl.ds(src_start, piece * bs)]
+        dst = out2.at[pl.ds(pl.multiple_of(c * bs, bs), bs), pl.ds(dst_start, piece * bs)]
+        if e == 0:
+            return pltpu.make_async_copy(src, dst, o2_send.at[e])
+        return pltpu.make_async_remote_copy(
+            src_ref=src,
+            dst_ref=dst,
+            send_sem=o2_send.at[e],
+            recv_sem=o2_recv.at[e],
+            device_id={"fac": f, "str": me},
+            device_id_type=MESH,
+        )
+
+    for e in reversed(range(nf)):
+
+        def finish(x, carry, e=e):
+            f = lax.rem(c + e, nf)
+            for y in range(piece // group):
+                sigma_two(f * half_blocks + x * piece + y * group)
+
+            @pl.when(x > 0)
+            def _():
+                piece_copy(e, x - 1).start()
+
+            return carry
+
+        lax.fori_loop(0, pieces, finish, 0)
+        piece_copy(e, pieces - 1).start()
+
+    for q in range(qc):
+        sent = send1[q].at[pl.ds(row_blocks, (n - 1) * row_blocks)]
+        pltpu.make_async_copy(sent, sent, send1_sem.at[q]).wait()
+        sent = send2[q].at[pl.ds(1, everyone - 1)]
+        pltpu.make_async_copy(sent, sent, send2_sem.at[q]).wait()
+        for e in range(nf):
+            share_copy(q, e).wait()
+    for e in range(nf):
+        sent = staged.at[:, pl.ds(0, half_blocks * bs)]
+        pltpu.make_async_copy(sent, sent, o2_send.at[e]).wait()
+        if e > 0:
+            pltpu.make_async_copy(sent, sent, o2_recv.at[e]).wait()
+
+
+def gather_factors(value):
+    count = lax.axis_size("fac")
+    me = lax.axis_index("fac")
+    shifted = [value]
+    for step in range(1, count):
+        pairs = [(x, (x + step) % count) for x in range(count)]
+        shifted.append(lax.ppermute(value, "fac", pairs))
+    whole = jnp.stack(shifted)
+    order = lax.rem(me - jnp.arange(count) + count, count)
+    return jnp.take(whole, order, axis=0)
+
+
+def split_body(
+    vector,
+    alpha_tiles,
+    alpha_pattern,
+    beta_tiles,
+    beta_pattern,
+    alpha_sector,
+    beta_sector,
+    alpha_diag,
+    beta_diag,
+    energy,
+):
+    n = lax.axis_size("str")
+    nf = lax.axis_size("fac")
+    sc, bs = alpha_tiles.shape[1], alpha_tiles.shape[2]
+    nab, nbb = alpha_sector.shape[0], beta_sector.shape[0]
+    qc = nbb // (n * nf)
+    kc = nf
+    tiles = gather_factors(jnp.stack([alpha_tiles[0], beta_tiles[0]]))
+    patterns = gather_factors(
+        jnp.concatenate([alpha_pattern.reshape(-1), beta_pattern.reshape(-1)])
+    )
+    ta = tiles[:, 0].reshape(kc * sc, bs, bs)
+    tb = tiles[:, 1].reshape(kc * sc * bs, bs)
+    pa = patterns[:, : nab * sc].reshape(-1)
+    pb = patterns[:, nab * sc :].reshape(-1)
+    rows = vector.shape[0]
+    me, c = lax.axis_index("str"), lax.axis_index("fac")
+    row_blocks = nab // n
+    pa_slot = lax.rem(me - pa // row_blocks + n, n) * row_blocks + lax.rem(pa, row_blocks)
+    pb_slot = (
+        lax.rem(pb, qc) * (n * nf)
+        + lax.rem(me - pb // (nf * qc) + n, n) * nf
+        + lax.rem(c - lax.rem(pb // qc, nf) + nf, nf)
+    )
+    live = (alpha_sector[:, None] == beta_sector[None, :]).astype(jnp.float32).reshape(-1)
+    vmem = pl.BlockSpec(memory_space=pltpu.VMEM)
+    smem = pl.BlockSpec(memory_space=pltpu.SMEM)
+    anywhere = pl.BlockSpec(memory_space=pl.ANY)
+    bf16 = jnp.bfloat16
+    first_update, second_update = pl.pallas_call(
+        functools.partial(exchange_kernel, (n, nf, bs, kc, sc, qc, nab, nbb)),
+        out_shape=(
+            jax.ShapeDtypeStruct((nab // nf, bs, nbb * bs // n), bf16),
+            jax.ShapeDtypeStruct((rows, nbb * bs // nf), bf16),
+        ),
+        in_specs=[anywhere] + [vmem] * 2 + [smem] * 5 + [vmem] * 2 + [smem],
+        out_specs=(anywhere, anywhere),
+        scratch_shapes=[
+            pltpu.VMEM((nbb, rows, bs), bf16),
+            [pltpu.VMEM((nab, kc, bs, bs), bf16) for _ in range(qc)],
+            [pltpu.VMEM((nab, kc, bs, bs), bf16) for _ in range(qc)],
+            [pltpu.VMEM((nab, bs, bs), bf16) for _ in range(qc)],
+            [pltpu.VMEM((n * nf, kc, bs, bs), bf16) for _ in range(qc)],
+            pltpu.VMEM((qc * n * nf, kc, bs, bs), bf16),
+            pltpu.VMEM((bs, nbb * bs), bf16),
+            pltpu.SemaphoreType.DMA((qc,)),
+            pltpu.SemaphoreType.DMA((qc,)),
+            pltpu.SemaphoreType.DMA((qc,)),
+            pltpu.SemaphoreType.DMA((qc,)),
+            pltpu.SemaphoreType.DMA((qc, nf)),
+            pltpu.SemaphoreType.DMA((qc, nf)),
+            pltpu.SemaphoreType.DMA((nf,)),
+            pltpu.SemaphoreType.DMA((nf,)),
+            pltpu.SemaphoreType.DMA,
+        ],
+        compiler_params=pltpu.CompilerParams(
+            collective_id=0, has_side_effects=True, vmem_limit_bytes=60 * 1024 * 1024
+        ),
+    )(
+        vector,
+        ta,
+        tb,
+        pa,
+        pa_slot,
+        pb,
+        pb_slot,
+        live,
+        alpha_diag.reshape(nab, bs),
+        beta_diag.reshape(nbb, bs),
+        energy,
+    )
+    return first_update.reshape(nab * bs // nf, nbb * bs // n), second_update
+
+
+def fits_split(*args):
+    vector, alpha_tiles, _, _, _, alpha_sector, beta_sector = args[:7]
+    n, nf = lax.axis_size("str"), lax.axis_size("fac")
+    bs = alpha_tiles.shape[2]
+    nab, nbb = alpha_sector.shape[0], beta_sector.shape[0]
+    return (
+        n > 1
+        and nf > 1
+        and alpha_tiles.shape[0] == 1
+        and bs % 128 == 0
+        and nab == n * nf
+        and nbb % (n * nf) == 0
+    )
+
+
+def either_body(*args):
+    return split_body(*args) if fits_split(*args) else body(*args)
+
+
 def solution(mesh):
     return jax.shard_map(
-        body,
+        either_body,
         mesh=mesh,
         in_specs=(
             P("str", None),

time: 489 us -> 216 us (0.44)
  Pallas kernels: 0 us -> 200 us
  waiting for transfers between devices: 143 us -> 0.01 us
  local copies, waits for them, and re-layouts: 133 us -> 11.4 us
  blocking collectives: 97.5 us -> 0 us
  other arithmetic: 56.5 us -> 2.22 us
  matrix products: 33.5 us -> 0 us
  between operations: 14.6 us -> 1.36 us
  starting transfers between devices: 7.05 us -> 0.82 us
    pallas_call x0 -> x1, Pallas kernels: none -> 200 us  [split_body(): pl.pallas_call(functools.partial(exchange_kernel, (n, nf, bs, kc, sc, qc,...]
    all_to_all x1 -> x0, blocking collectives: 97.5 us -> none  [body(): lax.all_to_all(back_image, 'str', split_axis=0, concat_axis=1, tiled=True)]
    all_to_all x1 -> x0, waiting for transfers between devices: 79.1 us -> none  [body(): lax.all_to_all(image, 'str', split_axis=1, concat_axis=0, tiled=True)]
    reduce_scatter x2 -> x0, waiting for transfers between devices: 49.1 us -> none  [the longest x1 31 us: body(): lax.psum_scatter(partial_value, 'fac', scatter_dimension=0, tiled=True)]
    select_n x6 -> x3, other arithmetic: 45.4 us -> 0.2 us  [gather_factors(): return jnp.take(whole, order, axis=0)]
    select_n x2 -> x0, local copies, waits for them, and re-layouts: 44.5 us -> none  [beta_apply(): jnp.take(blocks, pattern.reshape(-1), axis=1)]
    gather x4 -> x2, local copies, waits for them, and re-layouts: 44.9 us -> 1.21 us  [gather_factors(): return jnp.take(whole, order, axis=0)]
    dot_general x4 -> x0, matrix products: 33.5 us -> none  [the longest x2 21.8 us: beta_apply(): jnp.einsum('rjk,kc->rjc', picked, stacked, preferred_element_type=jnp.flo...]
  transfers between devices with their start and end apart: 4 -> 2, of which waited for: 4 -> 0; matrix products, arithmetic and copies ran while one was open for 0% -> 3% of each run, Pallas kernels for 0% -> 0%
where the time goes in v1:
time: 216 us
  Pallas kernels  200 us (93%)
  local copies, waits for them, and re-layouts  11.4 us (5%)
  other arithmetic  2.22 us (1%)
    pallas_call x1, Pallas kernels, split_body(): pl.pallas_call(functools.partial(exchange_kernel, (n, nf, bs, kc, sc, qc,...  200 us
    unnamed x12, local copies, waits for them, and re-layouts  6.99 us
  transfers between devices with their start and end apart: 2, of which 0 were waited for; matrix products, arithmetic and copies ran while one was open for 3% of the time, Pallas kernels for 0%

profile of v1, /device:TPU:3, one launch (start us, length us, event | category | flops | bytes accessed | tf_op | source)
XLA Modules:
  0.0 216.1 jit_solution(7858410493472467011)
XLA Ops:
  0.6 0.8 copy.13
  1.4 0.1 reshape.75
  1.5 0.8 copy.14
  2.3 0.1 reshape.76
  2.4 0.7 collective-permute-start.1
  3.2 0.9 constant_dynamic-update-slice_fusion.1
  4.1 0.9 constant_dynamic-update-slice_fusion
  5.0 0.1 collective-permute-start
  5.1 0.7 compare_convert_fusion
  6.5 0.7 reshape.82.live
  7.2 0.0 collective-permute-done.1
  7.2 0.6 gather_fusion.1
  7.8 0.1 broadcast_select_fusion.1
  7.9 0.5 slice_bitcast_fusion.1.pa
  8.4 0.6 fusion.10.pa_slot
  9.0 0.0 copy-start.1
  9.0 0.6 fusion.6.pb_slot
  9.6 0.0 collective-permute-done
  9.6 0.1 pad_maximum_fusion
  9.7 0.6 gather_fusion
  10.3 0.1 broadcast_select_fusion
  10.4 0.8 fusion.14
  11.3 0.0 copy-done.1
  11.3 200.3 %shard_map.113 = (bf16[16,128,512]{2,1,0:T(8,128)(2,1)}, bf16[256,4096]{1,0:T(8,128)(2,1)}) custom-call(bf16[256,8192]{1,0:T(8,128)(2,1)} %vec.1, bf16[8,128,128]{2,1,0:T(8,128)(2,1)} %bitcast.18, bf16[1024,128]{1,0:T(8,128)(2,1)} %bitcast.17, s32[256]{0:T(256)} %slice_bitcast_fusion.1.pa, s32[256]{0:T(256)} %fusion.10.pa_slot, s32[512]{0:T(512)} %bitcast.23, ...), custom_call_target="tpu_custom_call" | custom-call | tf_op jit(solution)/shard_map/pallas_call | solution.py:448
  211.5 0.0 copy-start
  211.5 3.2 %copy.22 = bf16[2048,512]{1,0:T(8,128)(2,1)} copy(bf16[2048,512]{1,0:T(8,128)(2,1)} %bitcast.16) | data formatting | bytes 4194304
  214.7 0.0 copy-done
  214.7 1.3 copy.23
  (11 shorter events, 0.1 us)
Async XLA Ops:
  2.4 4.8 %collective-permute-start.1 = (s32[384]{0:T(512)S(1)}, s32[384]{0:T(512)S(1)}, u32[]{:S(2)}, u32[]{:S(2)}) collective-permute-start(s32[384]{0:T(512)S(1)} %constant_dynamic-update-slice_fusion.3), channel_id=1, source_target_pairs={{0,16},{16,0},{1,17},{17,1},{2,18},{18,2},{3,19},{19,3},{4,20},{20... | collective-permute-start | bytes 4616 | tf_op jit(solution)/shard_map/ppermute | solution.py:402
  5.0 4.6 %collective-permute-start = (bf16[2,4,128,128]{3,2,1,0:T(8,128)(2,1)S(1)}, bf16[2,4,128,128]{3,2,1,0:T(8,128)(2,1)S(1)}, u32[]{:S(2)}, u32[]{:S(2)}) collective-permute-start(bf16[2,4,128,128]{3,2,1,0:T(8,128)(2,1)S(1)} %constant_dynamic-update-slice_fusion), channel_id=1, source_target_pairs={{0,16},{16,0},{1,17},{17,1},{2,18},{18,2},{3,19},{19,3},{4,20},{20... | collective-permute-start | bytes 786440 | tf_op jit(solution)/shard_map/ppermute | solution.py:402
  9.0 2.3 %copy-start.1 = (s32[1,2,2,128]{3,1,2,0:T(2,128)}, s32[1,2,2,128]{3,1,2,0:T(2,128)S(1)}, u32[]{:S(2)}) copy-start(s32[1,2,2,128]{3,1,2,0:T(2,128)S(1)} %copy.15) | copy-start | bytes 6148
  211.5 3.2 %copy-start = (bf16[256,4096]{1,0:T(8,128)(2,1)S(1)}, bf16[256,4096]{1,0:T(8,128)(2,1)}, u32[]{:S(2)}) copy-start(bf16[256,4096]{1,0:T(8,128)(2,1)} %get-tuple-element.11) | copy-start | bytes 6291460

commit v2 on v1

--- a/solution.py
+++ b/solution.py
@@ -132,6 +132,8 @@
     pb,
     pb_slot,
     live,
+    packed_rows,
+    packed_slot,
     adiag,
     bdiag,
     energy,
@@ -141,6 +143,9 @@
     send1,
     recv1,
     first,
+    packed,
+    mirrored,
+    expanded,
     send2,
     recv2,
     staged,
@@ -148,13 +153,17 @@
     recv1_sem,
     send2_sem,
     recv2_sem,
+    mirror_send,
+    mirror_recv,
     o1_send,
     o1_recv,
     o2_send,
     o2_recv,
     held_sem,
 ):
-    n, nf, bs, kc, sc, qc, nab, nbb = sizes
+    n, nf, bs, kc, sc, qc, nab, nbb, cap = sizes
+    hn = n // 2
+    team = hn * nf
     me = lax.axis_index("str")
     c = lax.axis_index("fac")
     everyone = n * nf
@@ -236,20 +245,63 @@
         beta_image(q, 0, recv1[q].at[pl.ds(0, row_blocks)])
         first_copy(q, n - 2).start()
 
+    half, inside = me // hn, lax.rem(me, hn)
+    mirror = lax.rem(me + hn, n)
+
+    def teammate(slot):
+        d = half * hn + lax.rem(inside + slot // nf, hn)
+        return d, lax.rem(c + lax.rem(slot, nf), nf)
+
     def second_slot(t):
-        return 1 + lax.rem(t + everyone // 2 - 1, everyone - 1)
-
-    def second_copy(q, t):
+        return 1 + lax.rem(t + team // 2 - 1, team - 1)
+
+    def second_copy(part, t):
         slot = second_slot(t)
-        d, f = partner(slot)
+        d, f = teammate(slot)
         return pltpu.make_async_remote_copy(
-            src_ref=send2[q].at[slot],
-            dst_ref=recv2.at[q * everyone + slot],
-            send_sem=send2_sem.at[q],
-            recv_sem=recv2_sem.at[q],
+            src_ref=send2[part].at[slot],
+            dst_ref=recv2.at[part * team + slot],
+            send_sem=send2_sem.at[part],
+            recv_sem=recv2_sem.at[part],
             device_id={"fac": f, "str": d},
             device_id_type=MESH,
         )
+
+    def mirror_copy(q):
+        return pltpu.make_async_remote_copy(
+            src_ref=packed[q],
+            dst_ref=mirrored[q],
+            send_sem=mirror_send.at[q],
+            recv_sem=mirror_recv.at[q],
+            device_id={"fac": c, "str": mirror},
+            device_id_type=MESH,
+        )
+
+    def spread_images(part, source):
+        def alpha_image(slot, dst):
+            d, f = teammate(slot)
+            i = d * nf + f
+            for k in range(kc):
+                picked = jnp.concatenate(
+                    [source[pa[(k * nab + i) * sc + s]] for s in range(sc)], axis=0
+                )
+                tiles = jnp.concatenate([ta[k * sc + s] for s in range(sc)], axis=1)
+                image = jnp.dot(tiles, picked, preferred_element_type=jnp.float32)
+                dst[k] = image.astype(jnp.bfloat16)
+
+        def step_two(t, carry):
+            slot = second_slot(t)
+            alpha_image(slot, send2[part].at[slot])
+
+            @pl.when(t > 0)
+            def _():
+                second_copy(part, t - 1).start()
+
+            return carry
+
+        lax.fori_loop(0, team - 1, step_two, 0)
+        alpha_image(0, recv2.at[part * team])
+        second_copy(part, team - 2).start()
 
     def share_copy(q, e):
         f = lax.rem(c + e, nf)
@@ -287,39 +339,31 @@
 
         lax.fori_loop(0, nab, sigma_one, 0)
 
-        def alpha_image(slot, dst, q=q):
-            d, f = partner(slot)
-            i = d * nf + f
-            for k in range(kc):
-                picked = jnp.concatenate(
-                    [
-                        first[q][pa[(k * nab + i) * sc + s]] for s in range(sc)
-                    ],
-                    axis=0,
-                )
-                tiles = jnp.concatenate([ta[k * sc + s] for s in range(sc)], axis=1)
-                image = jnp.dot(tiles, picked, preferred_element_type=jnp.float32)
-                dst[k] = image.astype(jnp.bfloat16)
-
-        def step_two(t, carry, q=q, alpha_image=alpha_image):
-            slot = second_slot(t)
-            alpha_image(slot, send2[q].at[slot])
-
-            @pl.when(t > 0)
-            def _():
-                second_copy(q, t - 1).start()
-
+        def pack(x, carry, q=q, j=j):
+            packed[q][x] = first[q][packed_rows[j * cap + x]]
             return carry
 
-        lax.fori_loop(0, everyone - 1, step_two, 0)
-        alpha_image(0, recv2.at[q * everyone])
-        second_copy(q, everyone - 2).start()
+        lax.fori_loop(0, cap, pack, 0)
+        mirror_copy(q).start()
+        spread_images(2 * q, first[q])
         for e in range(nf):
             share_copy(q, e).start()
 
     for q in range(qc):
-        landed = recv2.at[pl.ds(q * everyone + 1, everyone - 1)]
-        pltpu.make_async_copy(landed, landed, recv2_sem.at[q]).wait()
+        mirror_copy(q).wait_recv()
+        j = (mirror * nf + c) * qc + q
+
+        def expand(i, carry, q=q, j=j):
+            block = mirrored[q][packed_slot[j * nab + i]].astype(jnp.float32)
+            expanded[q][i] = (block * live[i * nbb + j]).astype(jnp.bfloat16)
+            return carry
+
+        lax.fori_loop(0, nab, expand, 0)
+        spread_images(2 * q + 1, expanded[q])
+
+    for part in range(2 * qc):
+        landed = recv2.at[pl.ds(part * team + 1, team - 1)]
+        pltpu.make_async_copy(landed, landed, recv2_sem.at[part]).wait()
 
     own = me * nf + c
     alpha_part = column(adiag, own)
@@ -382,8 +426,10 @@
     for q in range(qc):
         sent = send1[q].at[pl.ds(row_blocks, (n - 1) * row_blocks)]
         pltpu.make_async_copy(sent, sent, send1_sem.at[q]).wait()
-        sent = send2[q].at[pl.ds(1, everyone - 1)]
-        pltpu.make_async_copy(sent, sent, send2_sem.at[q]).wait()
+        for part in (2 * q, 2 * q + 1):
+            sent = send2[part].at[pl.ds(1, team - 1)]
+            pltpu.make_async_copy(sent, sent, send2_sem.at[part]).wait()
+        mirror_copy(q).wait_send()
         for e in range(nf):
             share_copy(q, e).wait()
     for e in range(nf):
@@ -435,34 +481,49 @@
     me, c = lax.axis_index("str"), lax.axis_index("fac")
     row_blocks = nab // n
     pa_slot = lax.rem(me - pa // row_blocks + n, n) * row_blocks + lax.rem(pa, row_blocks)
+    hn = n // 2
+    chip = pb // (nf * qc)
+    crossed = (chip // hn != me // hn).astype(jnp.int32)
     pb_slot = (
-        lax.rem(pb, qc) * (n * nf)
-        + lax.rem(me - pb // (nf * qc) + n, n) * nf
+        (lax.rem(pb, qc) * 2 + crossed) * (hn * nf)
+        + lax.rem(me - chip + n, hn) * nf
         + lax.rem(c - lax.rem(pb // qc, nf) + nf, nf)
     )
-    live = (alpha_sector[:, None] == beta_sector[None, :]).astype(jnp.float32).reshape(-1)
+    alive = alpha_sector[None, :] == beta_sector[:, None]
+    live = alive.T.astype(jnp.float32).reshape(-1)
+    index = jnp.arange(nab)
+    place = jnp.sum(
+        (alive[:, None, :] & (index[None, None, :] < index[None, :, None])).astype(jnp.int32),
+        axis=2,
+    )
+    most = jnp.max(jnp.sum(alive.astype(jnp.int32), axis=1))
     vmem = pl.BlockSpec(memory_space=pltpu.VMEM)
     smem = pl.BlockSpec(memory_space=pltpu.SMEM)
     anywhere = pl.BlockSpec(memory_space=pl.ANY)
     bf16 = jnp.bfloat16
-    first_update, second_update = pl.pallas_call(
-        functools.partial(exchange_kernel, (n, nf, bs, kc, sc, qc, nab, nbb)),
+    call = lambda cap, rows_of, slot_of, ident: pl.pallas_call(
+        functools.partial(exchange_kernel, (n, nf, bs, kc, sc, qc, nab, nbb, cap)),
         out_shape=(
             jax.ShapeDtypeStruct((nab // nf, bs, nbb * bs // n), bf16),
             jax.ShapeDtypeStruct((rows, nbb * bs // nf), bf16),
         ),
-        in_specs=[anywhere] + [vmem] * 2 + [smem] * 5 + [vmem] * 2 + [smem],
+        in_specs=[anywhere] + [vmem] * 2 + [smem] * 7 + [vmem] * 2 + [smem],
         out_specs=(anywhere, anywhere),
         scratch_shapes=[
             pltpu.VMEM((nbb, rows, bs), bf16),
             [pltpu.VMEM((nab, kc, bs, bs), bf16) for _ in range(qc)],
             [pltpu.VMEM((nab, kc, bs, bs), bf16) for _ in range(qc)],
             [pltpu.VMEM((nab, bs, bs), bf16) for _ in range(qc)],
-            [pltpu.VMEM((n * nf, kc, bs, bs), bf16) for _ in range(qc)],
+            [pltpu.VMEM((cap, bs, bs), bf16) for _ in range(qc)],
+            [pltpu.VMEM((cap, bs, bs), bf16) for _ in range(qc)],
+            [pltpu.VMEM((nab, bs, bs), bf16) for _ in range(qc)],
+            [pltpu.VMEM((n // 2 * nf, kc, bs, bs), bf16) for _ in range(2 * qc)],
             pltpu.VMEM((qc * n * nf, kc, bs, bs), bf16),
             pltpu.VMEM((bs, nbb * bs), bf16),
             pltpu.SemaphoreType.DMA((qc,)),
             pltpu.SemaphoreType.DMA((qc,)),
+            pltpu.SemaphoreType.DMA((2 * qc,)),
+            pltpu.SemaphoreType.DMA((2 * qc,)),
             pltpu.SemaphoreType.DMA((qc,)),
             pltpu.SemaphoreType.DMA((qc,)),
             pltpu.SemaphoreType.DMA((qc, nf)),
@@ -472,7 +533,7 @@
             pltpu.SemaphoreType.DMA,
         ],
         compiler_params=pltpu.CompilerParams(
-            collective_id=0, has_side_effects=True, vmem_limit_bytes=60 * 1024 * 1024
+            collective_id=ident, has_side_effects=True, vmem_limit_bytes=60 * 1024 * 1024
         ),
     )(
         vector,
@@ -483,9 +544,22 @@
         pb,
         pb_slot,
         live,
+        rows_of,
+        slot_of,
         alpha_diag.reshape(nab, bs),
         beta_diag.reshape(nbb, bs),
         energy,
+    )
+
+    def with_room(cap, ident):
+        chosen = alive[:, None, :] & (place[:, None, :] == jnp.arange(cap)[None, :, None])
+        rows_of = jnp.sum(jnp.where(chosen, index[None, None, :], 0), axis=2).reshape(-1)
+        slot_of = jnp.where(alive, place, 0).reshape(-1)
+        return call(cap, rows_of, slot_of, ident)
+
+    room = nab * 11 // 16
+    first_update, second_update = lax.cond(
+        most <= room, lambda: with_room(room, 0), lambda: with_room(nab, 1)
     )
     return first_update.reshape(nab * bs // nf, nbb * bs // n), second_update
 
@@ -496,7 +570,8 @@
     bs = alpha_tiles.shape[2]
     nab, nbb = alpha_sector.shape[0], beta_sector.shape[0]
     return (
-        n > 1
+        n > 2
+        and n % 2 == 0
         and nf > 1
         and alpha_tiles.shape[0] == 1
         and bs % 128 == 0

time: 216 us -> 223 us (1.032)
  the two profiles are of different devices: /device:TPU:3 before, /device:TPU:29 now
where the time goes in v2:
time: 223 us
  Pallas kernels  203 us (91%)
  local copies, waits for them, and re-layouts  11 us (5%)
  other arithmetic  5.92 us (3%)
    pallas_call x1, Pallas kernels, split_body(): pl.pallas_call(functools.partial(exchange_kernel, (n, nf, bs, kc, sc, qc,...  203 us
    unnamed x14, local copies, waits for them, and re-layouts  6.14 us
  transfers between devices with their start and end apart: 2, of which 0 were waited for; matrix products, arithmetic and copies ran while one was open for 3% of the time, Pallas kernels for 0%

profile of v2, /device:TPU:29, one launch (start us, length us, event | category | flops | bytes accessed | tf_op | source)
XLA Modules:
  0.0 222.7 jit_solution(11262988547262839582)
XLA Ops:
  0.6 0.8 copy.23
  1.4 0.1 reshape.139
  1.5 0.8 copy.24
  2.3 0.1 reshape.140
  2.4 0.7 collective-permute-start.1
  3.2 0.9 constant_dynamic-update-slice_fusion.1
  4.1 0.9 constant_dynamic-update-slice_fusion
  5.0 0.1 collective-permute-start
  5.1 0.8 convert_reduce_fusion
  6.0 0.8 broadcast_compare_fusion
  6.7 0.7 compare_convert_fusion
  7.5 0.0 copy-start.1
  7.5 0.0 copy-start.2
  7.5 0.1 and_convert_fusion
  7.7 0.6 reduce_max.9
  9.0 0.1 reshape.143
  9.0 0.0 collective-permute-done.1
  9.1 0.6 gather_fusion.1
  9.6 0.1 broadcast_select_fusion.3
  9.8 0.0 collective-permute-done
  9.8 0.1 pad_maximum_fusion
  9.9 0.6 gather_fusion
  10.6 0.1 broadcast_select_fusion.2
  10.7 0.0 copy-done.1
  10.7 0.0 copy-done.2
  10.7 208.3 %conditional.1 = (bf16[256,4096]{1,0:T(8,128)(2,1)}, bf16[2048,512]{1,0:T(8,128)(2,1)S(1)}) conditional(s32[]{:T(128)} %convert_element_type.20, (bf16[2,2,4,128,128]{4,3,2,1,0:T(8,128)(2,1)S(1)}, s32[256]{0:T(256)S(1)}, pred[256]{0:T(512)(128)(4,1)S(1)}, s32[256]{0:T(256)S(1)}, s32[512]{0:T(512)S(1)}, /*index=5*/s32[512]{0:T(512)S(1)}, ...), branch_computations={%region_2.5_spmd, %region_5.8_spmd} | conditional | flops 331776 | bytes 1444244 | solution.py:561
  10.7 0.5 fusion.11.pa_slot
  11.3 0.6 fusion.9.pb_slot
  11.9 0.1 copy.20
  12.0 1.2 reduce_sum.44
  13.1 0.1 copy.21
  13.2 0.2 select_reduce_fusion.1
  13.4 0.7 reshape.131.packed_slot
  14.0 0.1 copy.22
  14.1 0.7 reshape.130.packed_rows
  14.9 0.8 fusion.26
  15.7 203.3 %branch_1_fun.2 = (bf16[16,128,512]{2,1,0:T(8,128)(2,1)S(1)}, bf16[256,4096]{1,0:T(8,128)(2,1)}) custom-call(bf16[256,8192]{1,0:T(8,128)(2,1)} %get-tuple-element.279.vec, bf16[8,128,128]{2,1,0:T(8,128)(2,1)} %bitcast.31, bf16[1024,128]{1,0:T(8,128)(2,1)} %bitcast.30, s32[256]{0:T(256)S(1)} %get-tuple-element.281.pa, s32[256]{0:T(256)} %fusion.11.pa_slot, ...), custom_call_target="tpu_custom_call" | custom-call | tf_op jit(solution)/shard_map/cond/branch_1_fun/pallas_call | solution.py:504
  219.0 0.0 copy-start
  219.0 1.3 copy.41
  220.3 1.0 copy-done
  221.3 1.3 copy.42
  (23 shorter events, 0.2 us)
Async XLA Ops:
  2.4 6.6 %collective-permute-start.1 = (s32[384]{0:T(512)S(1)}, s32[384]{0:T(512)S(1)}, u32[]{:S(2)}, u32[]{:S(2)}) collective-permute-start(s32[384]{0:T(512)S(1)} %constant_dynamic-update-slice_fusion.3), channel_id=1, source_target_pairs={{0,16},{16,0},{1,17},{17,1},{2,18},{18,2},{3,19},{19,3},{4,20},{20... | collective-permute-start | bytes 4616 | tf_op jit(solution)/shard_map/ppermute | solution.py:448
  5.0 4.8 %collective-permute-start = (bf16[2,4,128,128]{3,2,1,0:T(8,128)(2,1)S(1)}, bf16[2,4,128,128]{3,2,1,0:T(8,128)(2,1)S(1)}, u32[]{:S(2)}, u32[]{:S(2)}) collective-permute-start(bf16[2,4,128,128]{3,2,1,0:T(8,128)(2,1)S(1)} %constant_dynamic-update-slice_fusion), channel_id=1, source_target_pairs={{0,16},{16,0},{1,17},{17,1},{2,18},{18,2},{3,19},{19,3},{4,20},{20... | collective-permute-start | bytes 786440 | tf_op jit(solution)/shard_map/ppermute | solution.py:448
  7.5 3.2 %copy-start.1 = (f32[8192]{0:T(1024)S(1)}, f32[8192]{0:T(1024)}, u32[]{:S(2)}) copy-start(f32[8192]{0:T(1024)} %param.20) | copy-start | bytes 98308
  7.5 3.2 %copy-start.2 = (f32[4096]{0:T(1024)S(1)}, f32[4096]{0:T(1024)}, u32[]{:S(2)}) copy-start(f32[4096]{0:T(1024)} %param.19) | copy-start | bytes 49156
  219.0 2.3 %copy-start = (bf16[256,4096]{1,0:T(8,128)(2,1)S(1)}, bf16[256,4096]{1,0:T(8,128)(2,1)}, u32[]{:S(2)}) copy-start(bf16[256,4096]{1,0:T(8,128)(2,1)} %get-tuple-element.420) | copy-start | bytes 6291460

commit v3 on v1

--- a/solution.py
+++ b/solution.py
@@ -162,6 +162,9 @@
     half_rows = nab // nf
     half_blocks = nbb // nf
 
+    def factor_of(k):
+        return lax.rem(c - k + nf, nf)
+
     def partner(slot):
         return lax.rem(me + slot // nf, n), lax.rem(c + lax.rem(slot, nf), nf)
 
@@ -200,7 +203,7 @@
             )
             image = jnp.dot(
                 picked,
-                tb[k * sc * bs : (k + 1) * sc * bs, :],
+                tb[k][...],
                 preferred_element_type=jnp.float32,
             )
             for x in range(row_blocks):
@@ -276,7 +279,7 @@
             for k in range(kc):
                 for s in range(sc):
                     parts.append(recv1[q][pa_slot[(k * nab + i) * sc + s], k])
-            tiles = jnp.concatenate([ta[x] for x in range(kc * sc)], axis=1)
+            tiles = jnp.concatenate([ta[k][s] for k in range(kc) for s in range(sc)], axis=1)
             sigma = jnp.dot(
                 tiles, jnp.concatenate(parts, axis=0), preferred_element_type=jnp.float32
             )
@@ -297,9 +300,9 @@
                     ],
                     axis=0,
                 )
-                tiles = jnp.concatenate([ta[k * sc + s] for s in range(sc)], axis=1)
+                tiles = jnp.concatenate([ta[k][s] for s in range(sc)], axis=1)
                 image = jnp.dot(tiles, picked, preferred_element_type=jnp.float32)
-                dst[k] = image.astype(jnp.bfloat16)
+                dst[factor_of(k)] = image.astype(jnp.bfloat16)
 
         def step_two(t, carry, q=q, alpha_image=alpha_image):
             slot = second_slot(t)
@@ -326,16 +329,17 @@
     group = 4 if half_blocks % 4 == 0 else 1
 
     def sigma_two(first_block):
+        stacked = jnp.concatenate([tb[k][...] for k in range(kc)], axis=0)
         rows = []
         for g in range(group):
             parts = []
             for k in range(kc):
                 for s in range(sc):
                     slot = pb_slot[(k * nbb + first_block + g) * sc + s]
-                    parts.append(recv2[slot, k])
+                    parts.append(recv2[slot, factor_of(k)])
             rows.append(jnp.concatenate(parts, axis=1))
         sigma = jnp.dot(
-            jnp.concatenate(rows, axis=0), tb[...], preferred_element_type=jnp.float32
+            jnp.concatenate(rows, axis=0), stacked, preferred_element_type=jnp.float32
         )
         for g in range(group):
             j = first_block + g
@@ -400,9 +404,7 @@
     for step in range(1, count):
         pairs = [(x, (x + step) % count) for x in range(count)]
         shifted.append(lax.ppermute(value, "fac", pairs))
-    whole = jnp.stack(shifted)
-    order = lax.rem(me - jnp.arange(count) + count, count)
-    return jnp.take(whole, order, axis=0)
+    return shifted
 
 
 def split_body(
@@ -423,12 +425,11 @@
     nab, nbb = alpha_sector.shape[0], beta_sector.shape[0]
     qc = nbb // (n * nf)
     kc = nf
-    tiles = gather_factors(jnp.stack([alpha_tiles[0], beta_tiles[0]]))
-    patterns = gather_factors(
+    ta = gather_factors(alpha_tiles[0])
+    tb = [x.reshape(sc * bs, bs) for x in gather_factors(beta_tiles[0])]
+    patterns = jnp.stack(gather_factors(
         jnp.concatenate([alpha_pattern.reshape(-1), beta_pattern.reshape(-1)])
-    )
-    ta = tiles[:, 0].reshape(kc * sc, bs, bs)
-    tb = tiles[:, 1].reshape(kc * sc * bs, bs)
+    ))
     pa = patterns[:, : nab * sc].reshape(-1)
     pb = patterns[:, nab * sc :].reshape(-1)
     rows = vector.shape[0]
@@ -451,7 +452,7 @@
             jax.ShapeDtypeStruct((nab // nf, bs, nbb * bs // n), bf16),
             jax.ShapeDtypeStruct((rows, nbb * bs // nf), bf16),
         ),
-        in_specs=[anywhere] + [vmem] * 2 + [smem] * 5 + [vmem] * 2 + [smem],
+        in_specs=[anywhere, [vmem] * nf, [vmem] * nf] + [smem] * 5 + [vmem] * 2 + [smem],
         out_specs=(anywhere, anywhere),
         scratch_shapes=[
             pltpu.VMEM((nbb, rows, bs), bf16),

time: 216 us -> 215 us (level)
  local copies, waits for them, and re-layouts: 11.4 us -> 7.65 us
    unnamed x12 -> x14, local copies, waits for them, and re-layouts: 6.99 us -> 6.75 us
  transfers between devices with their start and end apart: 2 -> 3, of which waited for: 0 -> 0; matrix products, arithmetic and copies ran while one was open for 3% -> 1% of each run, Pallas kernels for 0% -> 0%
where the time goes in v3:
time: 215 us
  Pallas kernels  202 us (94%)
  local copies, waits for them, and re-layouts  7.65 us (4%)
    pallas_call x1, Pallas kernels, split_body(): pl.pallas_call(functools.partial(exchange_kernel, (n, nf, bs, kc, sc, qc,...  202 us
    unnamed x14, local copies, waits for them, and re-layouts  6.75 us
  transfers between devices with their start and end apart: 3, of which 0 were waited for; matrix products, arithmetic and copies ran while one was open for 1% of the time, Pallas kernels for 0%

profile of v3, /device:TPU:3, one launch (start us, length us, event | category | flops | bytes accessed | tf_op | source)
XLA Modules:
  0.0 214.6 jit_solution(11414134110991458141)
XLA Ops:
  0.6 0.8 copy.13
  1.4 0.1 reshape.37
  1.5 0.8 copy.14
  2.3 0.1 reshape.38
  2.4 0.7 collective-permute-start.2
  3.2 0.1 collective-permute-start
  3.2 0.4 collective-permute-start.1
  3.7 0.7 compare_convert_fusion
  5.1 0.7 reshape.44.live
  5.7 0.0 collective-permute-done.2
  5.8 0.0 copy-start.3
  5.8 0.6 fusion.6.pb_slot
  6.4 0.6 fusion.11
  7.0 0.0 collective-permute-done.ta_1_
  7.0 0.0 copy-start.1
  7.0 0.0 collective-permute-done.1
  7.0 0.0 copy-start.2
  7.0 0.0 copy-done.3
  7.0 0.6 copy-done.1
  7.7 0.0 copy-done.2
  7.7 202.3 %shard_map.113 = (bf16[16,128,512]{2,1,0:T(8,128)(2,1)}, bf16[256,4096]{1,0:T(8,128)(2,1)}) custom-call(bf16[256,8192]{1,0:T(8,128)(2,1)} %vec.1, bf16[4,128,128]{2,1,0:T(8,128)(2,1)} %bitcast.15, bf16[4,128,128]{2,1,0:T(8,128)(2,1)} %copy-done.1, bf16[512,128]{1,0:T(8,128)(2,1)} %bitcast.17, bf16[512,128]{1,0:T(8,128)(2,1)} %bitcast.18, ...), custom_call_target="tpu_custom_call" | custom-call | tf_op jit(solution)/shard_map/pallas_call | solution.py:449
  210.0 0.0 copy-start
  210.1 3.2 %copy.21 = bf16[2048,512]{1,0:T(8,128)(2,1)} copy(bf16[2048,512]{1,0:T(8,128)(2,1)} %bitcast.13) | data formatting | bytes 4194304
  213.3 0.0 copy-done
  213.3 1.3 copy.22
  (7 shorter events, 0.1 us)
Async XLA Ops:
  2.4 3.3 %collective-permute-start.2 = (s32[384]{0:T(512)S(1)}, s32[384]{0:T(512)S(1)}, u32[]{:S(2)}, u32[]{:S(2)}) collective-permute-start(s32[384]{0:T(512)S(1)} %constant_dynamic-update-slice_fusion), channel_id=1, source_target_pairs={{0,16},{16,0},{1,17},{17,1},{2,18},{18,2},{3,19},{19,3},{4,20},{20... | collective-permute-start | bytes 4616 | tf_op jit(solution)/shard_map/ppermute | solution.py:406
  3.2 3.8 %collective-permute-start = (bf16[4,128,128]{2,1,0:T(8,128)(2,1)}, bf16[4,128,128]{2,1,0:T(8,128)(2,1)S(1)}, u32[]{:S(2)}, u32[]{:S(2)}) collective-permute-start(bf16[4,128,128]{2,1,0:T(8,128)(2,1)} %bitcast.14), channel_id=1, source_target_pairs={{0,16},{16,0},{1,17},{17,1},{2,18},{18,2},{3,19},{19,3},{4,20},{20... | collective-permute-start | bytes 393224 | tf_op jit(solution)/shard_map/ppermute | solution.py:406
  3.2 3.8 %collective-permute-start.1 = (bf16[4,128,128]{2,1,0:T(8,128)(2,1)}, bf16[4,128,128]{2,1,0:T(8,128)(2,1)S(1)}, u32[]{:S(2)}, u32[]{:S(2)}) collective-permute-start(bf16[4,128,128]{2,1,0:T(8,128)(2,1)} %bitcast.16), channel_id=1, source_target_pairs={{0,16},{16,0},{1,17},{17,1},{2,18},{18,2},{3,19},{19,3},{4,20},{20... | collective-permute-start | bytes 393224 | tf_op jit(solution)/shard_map/ppermute | solution.py:406
  5.8 1.3 copy-start.3
  7.0 0.7 copy-start.1
  7.0 0.7 copy-start.2
  210.0 3.2 %copy-start = (bf16[256,4096]{1,0:T(8,128)(2,1)S(1)}, bf16[256,4096]{1,0:T(8,128)(2,1)}, u32[]{:S(2)}) copy-start(bf16[256,4096]{1,0:T(8,128)(2,1)} %get-tuple-element.11) | copy-start | bytes 6291460

commit v4 on v3

--- a/solution.py
+++ b/solution.py
@@ -473,7 +473,7 @@
             pltpu.SemaphoreType.DMA,
         ],
         compiler_params=pltpu.CompilerParams(
-            collective_id=0, has_side_effects=True, vmem_limit_bytes=60 * 1024 * 1024
+            collective_id=0, has_side_effects=True, vmem_limit_bytes=32 * 1024 * 1024
         ),
     )(
         vector,

time: 215 us -> 214 us (level)
  local copies, waits for them, and re-layouts: 7.65 us -> 9.96 us
    unnamed x14 -> x16, local copies, waits for them, and re-layouts: 6.75 us -> 9.66 us
  transfers between devices with their start and end apart: 3 -> 3, of which waited for: 0 -> 0; matrix products, arithmetic and copies ran while one was open for 1% -> 0% of each run, Pallas kernels for 0% -> 0%
where the time goes in v4:
time: 214 us
  Pallas kernels  200 us (93%)
  local copies, waits for them, and re-layouts  9.96 us (5%)
    pallas_call x1, Pallas kernels, split_body(): pl.pallas_call(functools.partial(exchange_kernel, (n, nf, bs, kc, sc, qc,...  200 us
    unnamed x16, local copies, waits for them, and re-layouts  9.66 us
  transfers between devices with their start and end apart: 3, of which 0 were waited for; matrix products, arithmetic and copies ran while one was open for 0% of the time, Pallas kernels for 0%

profile of v4, /device:TPU:3, one launch (start us, length us, event | category | flops | bytes accessed | tf_op | source)
XLA Modules:
  0.0 213.6 jit_solution(14963504937089088666)
XLA Ops:
  0.6 0.8 copy.13
  1.4 0.1 reshape.37
  1.5 0.8 copy.14
  2.3 0.1 reshape.38
  2.4 0.7 collective-permute-start.2
  3.2 0.1 collective-permute-start
  3.2 0.4 collective-permute-start.1
  3.7 0.7 compare_convert_fusion
  5.1 0.1 reshape.44.live
  5.1 0.0 collective-permute-done.2
  5.2 0.0 collective-permute-done.ta_1_
  5.2 0.0 collective-permute-done.1
  5.2 0.0 copy-start
  5.3 2.2 %copy-done = bf16[256,8192]{1,0:T(8,128)(2,1)S(1)} copy-done((bf16[256,8192]{1,0:T(8,128)(2,1)S(1)}, bf16[256,8192]{1,0:T(8,128)(2,1)}, u32[]{:S(2)}) %copy-start) | copy-done | bytes 4194328
  7.4 0.0 copy-start.1
  7.4 0.9 copy-done.1
  8.3 0.0 copy-start.2
  8.3 0.9 copy-done.2
  9.2 0.0 copy-start.3
  9.2 0.8 copy-done.3
  10.0 0.0 copy-start.4
  10.0 0.7 copy-done.4
  10.7 200.2 %shard_map.113 = (bf16[16,128,512]{2,1,0:T(8,128)(2,1)S(1)}, bf16[256,4096]{1,0:T(8,128)(2,1)S(1)}) custom-call(bf16[256,8192]{1,0:T(8,128)(2,1)S(1)} %copy-done, bf16[4,128,128]{2,1,0:T(8,128)(2,1)S(1)} %bitcast.15, bf16[4,128,128]{2,1,0:T(8,128)(2,1)S(1)} %collective-permute-done.ta_1_, bf16[512,128]{1,0:T(8,128)(2,1)S(1)} %bitcast.17, ...), custom_call_target="tpu_custom_call" | custom-call | tf_op jit(solution)/shard_map/pallas_call | solution.py:449
  211.0 1.3 copy.21
  212.3 1.3 copy.22
  (9 shorter events, 0.1 us)
Async XLA Ops:
  2.4 2.7 %collective-permute-start.2 = (s32[384]{0:T(512)S(1)}, s32[384]{0:T(512)S(1)}, u32[]{:S(2)}, u32[]{:S(2)}) collective-permute-start(s32[384]{0:T(512)S(1)} %constant_dynamic-update-slice_fusion), channel_id=1, source_target_pairs={{0,16},{16,0},{1,17},{17,1},{2,18},{18,2},{3,19},{19,3},{4,20},{20... | collective-permute-start | bytes 4616 | tf_op jit(solution)/shard_map/ppermute | solution.py:406
  3.2 2.1 collective-permute-start
  3.2 2.0 collective-permute-start.1
  5.2 2.2 %copy-start = (bf16[256,8192]{1,0:T(8,128)(2,1)S(1)}, bf16[256,8192]{1,0:T(8,128)(2,1)}, u32[]{:S(2)}) copy-start(bf16[256,8192]{1,0:T(8,128)(2,1)} %vec.1) | copy-start | bytes 12582916
  7.4 0.9 copy-start.1
  8.3 0.9 copy-start.2
  9.2 0.8 copy-start.3
  10.0 0.7 copy-start.4
